TPU v7x, 256 devices: a whole 4x4x8 slice. The times are simulated.
256 devices in a mesh: seq: 64 (over y, z_lo, x), mp: 4 (over z_hi, core).
Axes of the slice: x: 4, y: 4, z: 8 (z_hi: 2, z_lo: 4; z = z_hi * 4 + z_lo), core: 2. Of those that a mesh axis runs over, the one named last changes fastest.
Arguments:
- projected: bfloat16 [3, 8192, 8192], P(None, 'mp', 'seq'), may hold values from -6 to 6
- short_taps: float32 [3, 3, 8192], replicated, may hold values from -4 to 4
- skip_gain: float32 [8192], replicated, may hold values from -4 to 4
- residue: float32 [2048, 16], P('seq'), may hold values from -4 to 4
- decay_rate: float32 [2048, 16], P('seq'), may hold values from 6.1035156e-05 to 0.05
Outputs:
- gated: bfloat16 [8192, 8192], P('mp', 'seq')
All inputs are finite; a program needn't handle non-finite values.
Results may differ from a plain program's by a relative error of at most 0.012.
Values may be sent and summed in bfloat16 or wider, within the bound.
No kernel may reach another device: no remote copies, remote signals or barrier semaphores. Data moves between devices by JAX's collectives and lax.ppermute only.
A program may use at most 128 MiB of HBM per device.

v0:
```python
import math
import jax
import jax.numpy as jnp
from jax import lax
from jax.sharding import PartitionSpec as P

exact_mode = lax.Precision.HIGHEST
full_turn = 2.0 * math.pi


def unit_table(row_count, column_count, period):
    indices = lax.broadcasted_iota(jnp.int32, (row_count, column_count), 0) * lax.broadcasted_iota(
        jnp.int32, (row_count, column_count), 1
    )
    angles = -full_turn / period * (indices % period).astype(jnp.float32)
    return (jnp.cos(angles), jnp.sin(angles))


def dft_tables(length):
    padded_len = 2 * length
    narrow = padded_len // 128
    outer_table = unit_table(128, 128, 128)
    twiddle = unit_table(128, narrow, padded_len)
    inner_table = unit_table(narrow, narrow, narrow)
    return (outer_table, twiddle, inner_table)


def forward(signal, tables):
    outer_table, twiddle, inner_table = tables
    signal_count = signal.shape[0]
    narrow = inner_table[0].shape[0]
    blocks = signal.reshape(signal_count, 64, narrow)
    section_re = jnp.einsum("ca,mab->mcb", outer_table[0][:, :64], blocks, precision=exact_mode)
    section_im = jnp.einsum("ca,mab->mcb", outer_table[1][:, :64], blocks, precision=exact_mode)
    turned_re = section_re * twiddle[0] - section_im * twiddle[1]
    turned_im = section_re * twiddle[1] + section_im * twiddle[0]
    spec_re = jnp.einsum(
        "mcb,bd->mcd", turned_re, inner_table[0], precision=exact_mode
    ) - jnp.einsum("mcb,bd->mcd", turned_im, inner_table[1], precision=exact_mode)
    spec_im = jnp.einsum(
        "mcb,bd->mcd", turned_re, inner_table[1], precision=exact_mode
    ) + jnp.einsum("mcb,bd->mcd", turned_im, inner_table[0], precision=exact_mode)
    return (spec_re, spec_im)


def inverse(spec_re, spec_im, tables):
    outer_table, twiddle, inner_table = tables
    signal_count = spec_re.shape[0]
    narrow = inner_table[0].shape[0]
    back_re = jnp.einsum("mcd,bd->mcb", spec_re, inner_table[0], precision=exact_mode) + jnp.einsum(
        "mcd,bd->mcb", spec_im, inner_table[1], precision=exact_mode
    )
    back_im = jnp.einsum("mcd,bd->mcb", spec_im, inner_table[0], precision=exact_mode) - jnp.einsum(
        "mcd,bd->mcb", spec_re, inner_table[1], precision=exact_mode
    )
    turned_re = back_re * twiddle[0] + back_im * twiddle[1]
    turned_im = back_im * twiddle[0] - back_re * twiddle[1]
    result = jnp.einsum(
        "ca,mcb->mab", outer_table[0][:, :64], turned_re, precision=exact_mode
    ) + jnp.einsum("ca,mcb->mab", outer_table[1][:, :64], turned_im, precision=exact_mode)
    return result.reshape(signal_count, 64 * narrow) / (128.0 * narrow)


def filter_kernel(residue, decay_rate, length):
    positions = lax.broadcasted_iota(jnp.float32, (1, length), 1)

    def add_term(state_index, kernel):
        rates = lax.dynamic_slice_in_dim(decay_rate, state_index, 1, 1)
        weight = lax.dynamic_slice_in_dim(residue, state_index, 1, 1) * jnp.sqrt(rates)
        return kernel + weight * jnp.exp(-rates * positions)

    return lax.fori_loop(
        0, residue.shape[1], add_term, jnp.zeros((residue.shape[0], length), jnp.float32)
    )


def long_convolve(product, residue, decay_rate):
    signal_count, length = product.shape
    tables = dft_tables(length)
    signal_re, signal_im = forward(product.astype(jnp.float32), tables)
    mp_count = lax.axis_size("mp")
    per_group = signal_count // mp_count
    local_residue = lax.dynamic_slice_in_dim(
        residue, lax.axis_index("mp") * per_group, per_group, 0
    )
    local_rate = lax.dynamic_slice_in_dim(
        decay_rate, lax.axis_index("mp") * per_group, per_group, 0
    )
    kernel_re, kernel_im = forward(filter_kernel(local_residue, local_rate, length), tables)
    grouped_shape = (mp_count, per_group) + signal_re.shape[1:]
    signal_re = signal_re.reshape(grouped_shape)
    signal_im = signal_im.reshape(grouped_shape)
    kernel_re = kernel_re[None]
    kernel_im = kernel_im[None]
    mixed_re = (signal_re * kernel_re - signal_im * kernel_im).reshape(
        (signal_count,) + signal_re.shape[-2:]
    )
    mixed_im = (signal_re * kernel_im + signal_im * kernel_re).reshape(
        (signal_count,) + signal_re.shape[-2:]
    )
    return inverse(mixed_re, mixed_im, tables).astype(jnp.bfloat16)


def to_channels(streams):
    stream_count, chan_width, row_count = streams.shape
    seq_count = lax.axis_size("seq")
    mp_count = lax.axis_size("mp")
    arranged = streams.reshape(
        stream_count, seq_count, mp_count, chan_width // (seq_count * mp_count), row_count
    )
    arrived = lax.all_to_all(
        lax.all_to_all(arranged, "seq", split_axis=1, concat_axis=4, tiled=True),
        "mp",
        split_axis=2,
        concat_axis=2,
        tiled=True,
    )
    return arrived.reshape(stream_count, chan_width // seq_count, row_count * seq_count)


def from_channels(values):
    chan_dev, length = values.shape
    seq_count = lax.axis_size("seq")
    mp_count = lax.axis_size("mp")
    arranged = values.reshape(1, mp_count, chan_dev // mp_count, length)
    arrived = lax.all_to_all(
        lax.all_to_all(arranged, "seq", split_axis=3, concat_axis=0, tiled=True),
        "mp",
        split_axis=1,
        concat_axis=1,
        tiled=True,
    )
    return arrived.reshape(seq_count * chan_dev, length // seq_count)


def chosen_channels(full, chan_dev, chan_width):
    model_index = lax.axis_index("mp")
    seq_index = lax.axis_index("seq")
    mp_count = lax.axis_size("mp")
    piece_size = chan_dev // mp_count
    grouped = full.reshape(full.shape[:-1] + (mp_count, chan_width))
    selected = lax.dynamic_slice_in_dim(
        grouped, seq_index * chan_dev + model_index * piece_size, piece_size, grouped.ndim - 1
    )
    return selected.reshape(full.shape[:-1] + (chan_dev,))


def short_convolve(extended, tap_block):
    return (
        tap_block[0][:, :, None] * extended[:, :, 2:]
        + tap_block[1][:, :, None] * extended[:, :, 1:-1]
        + tap_block[2][:, :, None] * extended[:, :, :-2]
    )


def body(projected, short_taps, skip_gain, residue, decay_rate):
    chan_width = projected.shape[1]
    chan_dev = chan_width // lax.axis_size("seq")
    streams = to_channels(projected)
    taps_here = chosen_channels(short_taps, chan_dev, chan_width)
    skip_here = chosen_channels(skip_gain, chan_dev, chan_width)
    extended = jnp.pad(streams.astype(jnp.float32), ((0, 0), (0, 0), (2, 0)))
    mixed = short_convolve(extended, taps_here)
    product = (mixed[1] * mixed[2]).astype(jnp.bfloat16)
    long_part = long_convolve(product, residue, decay_rate)
    total = long_part.astype(jnp.float32) + skip_here[:, None] * product.astype(jnp.float32)
    return from_channels((mixed[0] * total).astype(jnp.bfloat16))


def solution(mesh):
    in_specs = (P(None, "mp", "seq"), P(), P(), P("seq", None), P("seq", None))
    out_specs = P("mp", "seq")
    return jax.shard_map(body, mesh=mesh, in_specs=in_specs, out_specs=out_specs, check_vma=False)
```

profile of v0, /device:TPU:33, one launch (start us, length us, event | category | flops | bytes accessed | tf_op | source)
XLA Modules:
  0.0 227.2 jit_solution(2267840420173184764)
XLA Ops:
  0.0 2.8 %copy.98 = bf16[3,64,4,8,128]{4,3,2,0,1:T(8,128)(2,1)} copy(bf16[3,64,4,8,128]{4,3,2,1,0:T(8,128)(2,1)} %bitcast.146) | data formatting | bytes 3145728 | tf_op jit(solution)/shard_map/reshape | solution.py:108
  2.8 11.2 %all-to-all-start = ((bf16[3,64,4,8,128]{4,3,2,0,1:T(8,128)(2,1)}), bf16[3,64,4,8,128]{4,3,2,0,1:T(8,128)(2,1)S(1)}, u32[]{:S(2)}, u32[]{:S(2)}) async-start(bf16[3,64,4,8,128]{4,3,2,0,1:T(8,128)(2,1)} %copy.98), calls=%async_computation | async-start | bytes 3145728 | tf_op jit(solution)/shard_map/all_to_all | solution.py:112
  14.2 36.9 %all-to-all-done = bf16[3,64,4,8,128]{4,3,2,0,1:T(8,128)(2,1)S(1)} async-done(((bf16[3,64,4,8,128]{4,3,2,0,1:T(8,128)(2,1)}), bf16[3,64,4,8,128]{4,3,2,0,1:T(8,128)(2,1)S(1)}, u32[]{:S(2)}, u32[]{:S(2)}) %all-to-all-start) | async-done | bytes 1572896 | tf_op jit(solution)/shard_map/all_to_all | solution.py:112
  53.8 7.2 %all-to-all-start.1 = ((bf16[3,1,4,8,8192]{4,3,0,1,2:T(8,128)(2,1)}), bf16[3,1,4,8,8192]{4,3,0,1,2:T(8,128)(2,1)S(1)}, u32[]{:S(2)}, u32[]{:S(2)}) async-start(bf16[3,1,4,8,8192]{4,3,0,1,2:T(8,128)(2,1)} %reshape.166), calls=%async_computation.1 | async-start | bytes 3145728 | tf_op jit(solution)/shard_map/all_to_all | solution.py:111
  61.0 3.3 %while.14 = (s32[]{:T(128)}, f32[8,8192]{1,0:T(8,128)S(1)}, f32[8,16]{0,1:T(8,128)S(1)}, f32[8,16]{0,1:T(8,128)S(1)}, s32[]{:T(128)}, /*index=5*/s32[]{:T(128)}) while((s32[]{:T(128)}, f32[8,8192]{1,0:T(8,128)S(1)}, f32[8,16]{0,1:T(8,128)S(1)}, f32[8,16]{0,1:T(8,128)S(1)}, s32[]{:T(128)}, /*index=5*/s32[]{:T(128)}) %tuple.40), condition=%wide.region_1.2_spmd.clone, body=%wide.region_0.1_spmd.clone.sunk | while | flops 262163 | bytes 524571 | solution.py:72
  74.3 26.5 %all-to-all-done.1 = bf16[3,1,4,8,8192]{4,3,0,1,2:T(8,128)(2,1)S(1)} async-done(((bf16[3,1,4,8,8192]{4,3,0,1,2:T(8,128)(2,1)}), bf16[3,1,4,8,8192]{4,3,0,1,2:T(8,128)(2,1)S(1)}, u32[]{:S(2)}, u32[]{:S(2)}) %all-to-all-start.1) | async-done | bytes 1572896 | tf_op jit(solution)/shard_map/all_to_all | solution.py:111
  105.7 3.6 %fusion.44 = f32[32,128,128]{2,1,0:T(8,128)S(1)} fusion(f32[32,128,128]{2,1,0:T(8,128)S(1)} %fusion.92, f32[32,128,128]{2,1,0:T(8,128)S(1)} %fusion.91, f32[128,128]{0,1:T(8,128)S(1)} %get-tuple-element.132, f32[128,128]{0,1:T(8,128)S(1)} %get-tuple-element.133), kind=kOutput, calls=%fused_computation.55 | convolution fusion | flops 807108608 | bytes 6422528 | tf_op jit(solution)/shard_map/mcb,bd->mcd/dot_general | solution.py:37
  109.4 3.6 %fusion.42 = f32[32,128,128]{2,1,0:T(8,128)S(1)} fusion(f32[32,128,128]{2,1,0:T(8,128)S(1)} %fusion.92, f32[32,128,128]{2,1,0:T(8,128)S(1)} %fusion.91, f32[128,128]{0,1:T(8,128)S(1)} %get-tuple-element.132, f32[128,128]{0,1:T(8,128)S(1)} %get-tuple-element.133), kind=kOutput, calls=%fused_computation.54 | convolution fusion | flops 807108608 | bytes 6422528 | tf_op jit(solution)/shard_map/mcb,bd->mcd/dot_general | solution.py:40
  113.0 3.6 %convolution_subtract_fusion.1 = f32[32,128,128]{2,1,0:T(8,128)S(1)} fusion(f32[32,128,128]{2,1,0:T(8,128)S(1)} %fusion.44, f32[32,128,128]{2,1,0:T(8,128)S(1)} %fusion.92, f32[32,128,128]{2,1,0:T(8,128)S(1)} %fusion.91, f32[128,128]{0,1:T(8,128)S(1)} %get-tuple-element.132, f32[128,128]{0,1:T(8,128)S(1)} %get-tuple-element.133), kind=kOutput, calls=%fused_computation.32 | convolution fusion | flops 807632896 | bytes 8519680 | tf_op jit(solution)/shard_map/mcb,bd->mcd/dot_general | solution.py:39
  116.7 4.0 %fusion.6 = (f32[32,128,128]{2,1,0:T(8,128)S(1)}, f32[32,128,128]{2,1,0:T(8,128)S(1)}) fusion(f32[32,128,128]{2,1,0:T(8,128)S(1)} %convolution_subtract_fusion.1, f32[8,128,128]{2,1,0:T(8,128)S(1)} %copy-done, f32[8,128,128]{2,1,0:T(8,128)S(1)} %copy-done.1, f32[32,128,128]{2,1,0:T(8,128)S(1)} %fusion.42, f32[32,128,128]{2,1,0:T(8,128)S(1)} %fusion.92, ...), kind=kOutput, calls=%fused_computation.14 | convolution fusion | flops 810778624 | bytes 13762560 | tf_op jit(solution)/shard_map/mcb,bd->mcd/dot_general | solution.py:42
  120.7 2.3 fusion.62
  123.0 2.3 %fusion.60 = f32[32,128,128]{1,2,0:T(8,128)S(1)} fusion(f32[32,128,128]{2,1,0:T(8,128)S(1)} %get-tuple-element.127), kind=kOutput, calls=%fused_computation.77 | convolution fusion | flops 805535744 | bytes 4194304 | tf_op jit(solution)/shard_map/mcd,bd->mcb/dot_general | solution.py:53
  125.3 2.3 convolution_add_fusion
  127.5 2.5 %convolution_subtract_fusion = f32[32,128,128]{1,2,0:T(8,128)S(1)} fusion(f32[32,128,128]{1,2,0:T(8,128)S(1)} %fusion.60, f32[32,128,128]{2,1,0:T(8,128)S(1)} %get-tuple-element.128), kind=kOutput, calls=%fused_computation.29 | convolution fusion | flops 806060032 | bytes 6291456 | tf_op jit(solution)/shard_map/mcd,bd->mcb/dot_general | solution.py:53
  130.1 2.6 %fusion.9 = f32[32,128,64]{1,2,0:T(8,128)S(1)} fusion(f32[32,128,128]{1,2,0:T(8,128)S(1)} %convolution_add_fusion, f32[32,128,128]{1,2,0:T(8,128)S(1)} %convolution_subtract_fusion, f32[128,128]{0,1:T(8,128)S(1)} %get-tuple-element.132, f32[128,128]{0,1:T(8,128)S(1)} %get-tuple-element.133, f32[128,128]{0,1:T(8,128)S(1)} %fusion.77), kind=kOutput, calls=%fused_computation.21 | convolution fusion | flops 404226048 | bytes 5406720 | tf_op jit(solution)/shard_map/ca,mcb->mab/dot_general | solution.py:60
  132.7 3.6 %fusion.29 = f32[32,64,128]{2,1,0:T(8,128)} fusion(f32[32,128,64]{1,2,0:T(8,128)S(1)} %fusion.9, f32[32,128,128]{1,2,0:T(8,128)S(1)} %convolution_subtract_fusion, f32[32,128,128]{1,2,0:T(8,128)S(1)} %convolution_add_fusion, f32[128,128]{0,1:T(8,128)S(1)} %get-tuple-element.132, f32[128,128]{0,1:T(8,128)S(1)} %get-tuple-element.133, f32[128,128]{0,1:T(8,128)S(1)} %fusion.78), kind=kOutput, calls=%fused_computation.38 | convolution fusion | flops 405274624 | bytes 6455296 | tf_op jit(solution)/shard_map/ca,mcb->mab/dot_general | solution.py:58
  136.4 2.4 %reshape.150 = f32[1,4,8,8192]{3,2,1,0:T(8,128)} reshape(f32[32,64,128]{2,1,0:T(8,128)} %fusion.29) | data formatting | bytes 2097152 | tf_op jit(solution)/shard_map/convert_element_type | solution.py:166
  138.8 2.2 fusion.34
  141.0 9.6 %copy.130 = bf16[1,4,8,8192]{2,1,0,3:T(4,128)(2,1)} copy(bf16[1,4,8,8192]{3,2,1,0:T(8,128)(2,1)} %fusion.34) | data formatting | bytes 1048576 | tf_op jit(solution)/shard_map/convert_element_type | solution.py:167
  150.6 10.5 %reshape.167 = bf16[64,2,2048]{2,1,0:T(2,128)(2,1)S(1)} reshape(bf16[8192,1,4,8]{3,2,1,0:T(4,128)(2,1)} %bitcast.138) | data formatting | bytes 1048576
  161.1 20.9 %all_to_all.46 = bf16[64,2,2048]{2,1,0:T(2,128)(2,1)S(1)} all-to-all(bf16[64,2,2048]{2,1,0:T(2,128)(2,1)S(1)} %reshape.167), channel_id=1, replica_groups=mesh['seq'=64,'mp'=4] {'seq'}, dimensions={0} | all-to-all | bytes 1048576 | tf_op jit(solution)/shard_map/all_to_all | solution.py:127
  182.0 10.9 %reshape.168 = bf16[8192,1,4,8]{3,2,1,0:T(4,128)(2,1)} reshape(bf16[64,2,2048]{2,1,0:T(2,128)(2,1)S(1)} %all_to_all.46) | data formatting | bytes 1048576
  192.9 9.9 %copy.131 = bf16[1,4,8,64,128]{4,2,3,1,0:T(8,128)(2,1)S(1)} copy(bf16[1,4,8,64,128]{2,1,4,3,0:T(4,128)(2,1)} %bitcast.139) | data formatting | bytes 1048576 | tf_op jit(solution)/shard_map/all_to_all | solution.py:127
  202.8 23.2 %all_to_all.47 = bf16[64,4,8,128]{3,2,0,1:T(8,128)(2,1)S(1)} all-to-all(bf16[64,4,8,128]{3,2,0,1:T(8,128)(2,1)S(1)} %bitcast.145), channel_id=1, replica_groups=mesh['seq'=64,'mp'=4] {'mp'}, dimensions={1} | all-to-all | bytes 1048576 | tf_op jit(solution)/shard_map/all_to_all | solution.py:126
  (71 shorter events, 20.7 us)
Async XLA Ops:
  2.8 11.3 %copy-start.4 = (f32[32,16]{0,1:T(8,128)S(1)}, f32[32,16]{0,1:T(8,128)}, u32[]{:S(2)}) copy-start(f32[32,16]{0,1:T(8,128)} %param.11) | copy-start | bytes 6148
  2.8 11.3 %copy-start.5 = (f32[32,16]{0,1:T(8,128)S(1)}, f32[32,16]{0,1:T(8,128)}, u32[]{:S(2)}) copy-start(f32[32,16]{0,1:T(8,128)} %param.10) | copy-start | bytes 6148
  2.8 48.3 %all-to-all-start = ((bf16[3,64,4,8,128]{4,3,2,0,1:T(8,128)(2,1)}), bf16[3,64,4,8,128]{4,3,2,0,1:T(8,128)(2,1)S(1)}, u32[]{:S(2)}, u32[]{:S(2)}) async-start(bf16[3,64,4,8,128]{4,3,2,0,1:T(8,128)(2,1)} %copy.98), calls=%async_computation | async-start | bytes 3145728 | tf_op jit(solution)/shard_map/all_to_all | solution.py:112
  53.8 47.1 %all-to-all-start.1 = ((bf16[3,1,4,8,8192]{4,3,0,1,2:T(8,128)(2,1)}), bf16[3,1,4,8,8192]{4,3,0,1,2:T(8,128)(2,1)S(1)}, u32[]{:S(2)}, u32[]{:S(2)}) async-start(bf16[3,1,4,8,8192]{4,3,0,1,2:T(8,128)(2,1)} %reshape.166), calls=%async_computation.1 | async-start | bytes 3145728 | tf_op jit(solution)/shard_map/all_to_all | solution.py:111
  61.0 3.3 %copy-start.2 = (f32[3,3,8192]{2,1,0:T(4,128)S(1)}, f32[3,3,8192]{2,1,0:T(4,128)}, u32[]{:S(2)}) copy-start(f32[3,3,8192]{2,1,0:T(4,128)} %param.8) | copy-start | bytes 884740
  61.0 3.9 %copy-start.3 = (f32[8192]{0:T(1024)S(1)}, f32[8192]{0:T(1024)}, u32[]{:S(2)}) copy-start(f32[8192]{0:T(1024)} %param.9) | copy-start | bytes 98308
  113.0 3.7 %copy-start = (f32[8,128,128]{2,1,0:T(8,128)S(1)}, f32[8,128,128]{2,1,0:T(8,128)}, u32[]{:S(2)}) copy-start(f32[8,128,128]{2,1,0:T(8,128)} %convolution_add_fusion.2) | copy-start | bytes 1572868
  113.0 3.7 %copy-start.1 = (f32[8,128,128]{2,1,0:T(8,128)S(1)}, f32[8,128,128]{2,1,0:T(8,128)}, u32[]{:S(2)}) copy-start(f32[8,128,128]{2,1,0:T(8,128)} %convolution_subtract_fusion.2) | copy-start | bytes 1572868
where the time goes:
time: 231 us; the launch traced here: 227 us
  waiting for transfers between devices  63.5 us (27%)
  local copies, waits for them, and re-layouts  50.6 us (22%)
  blocking collectives  44.1 us (19%)
  matrix products  41.5 us (18%)
  starting transfers between devices  18.4 us (8%)
  other arithmetic  7.44 us (3%)
    all_to_all x1, waiting for transfers between devices, to_channels(): lax.all_to_all(arranged, 'seq', split_axis=1, concat_axis=4, tiled=True)  36.9 us
    all_to_all x1, waiting for transfers between devices, to_channels(): lax.all_to_all(lax.all_to_all(arranged, 'seq', split_axis=1, concat_axis=...  26.5 us
    all_to_all x1, blocking collectives, from_channels(): lax.all_to_all(lax.all_to_all(arranged, 'seq', split_axis=3, concat_axis=...  23.2 us
    unnamed x15, local copies, waits for them, and re-layouts  21.5 us
    all_to_all x1, blocking collectives, from_channels(): lax.all_to_all(arranged, 'seq', split_axis=3, concat_axis=0, tiled=True)  20.9 us
    all_to_all x1, starting transfers between devices, to_channels(): lax.all_to_all(arranged, 'seq', split_axis=1, concat_axis=4, tiled=True)  11.2 us
    all_to_all x1, local copies, waits for them, and re-layouts, from_channels(): lax.all_to_all(arranged, 'seq', split_axis=3, concat_axis=0, tiled=True)  9.86 us
    convert_element_type x1, local copies, waits for them, and re-layouts, body(): return from_channels((mixed[0] * total).astype(jnp.bfloat16))  9.63 us
  transfers between devices with their start and end apart: 2, of which 2 were waited for; matrix products, arithmetic and copies ran while one was open for 5% of the time, Pallas kernels for 0%

commit v1 on v0

--- a/solution.py
+++ b/solution.py
@@ -3,6 +3,7 @@
 import jax.numpy as jnp
 from jax import lax
 from jax.sharding import PartitionSpec as P
+from jax.lax import all_to_all, axis_size
 
 exact_mode = lax.Precision.HIGHEST
 full_turn = 2.0 * math.pi
@@ -123,12 +124,17 @@
     seq_count = lax.axis_size("seq")
     mp_count = lax.axis_size("mp")
     arranged = values.reshape(1, mp_count, chan_dev // mp_count, length)
+    arrange_map_over_axis = lambda arr_in, dim_i, dim_at: jnp.concatenate(
+        all_to_all(
+            jnp.stack(jnp.split(arr_in, axis_size("seq"), axis=dim_at)),
+            axis_name="seq",
+            split_axis=0,
+            concat_axis=0,
+        ),
+        axis=dim_i,
+    )
     arrived = lax.all_to_all(
-        lax.all_to_all(arranged, "seq", split_axis=3, concat_axis=0, tiled=True),
-        "mp",
-        split_axis=1,
-        concat_axis=1,
-        tiled=True,
+        arrange_map_over_axis(arranged, 0, 3), "mp", split_axis=1, concat_axis=1, tiled=True
     )
     return arrived.reshape(seq_count * chan_dev, length // seq_count)
 

time: 231 us -> 189 us (0.82)
  local copies, waits for them, and re-layouts: 50.6 us -> 10.6 us
    unnamed x15 -> x76, local copies, waits for them, and re-layouts: 21.5 us -> 0.86 us
    all_to_all x2 -> x1, local copies, waits for them, and re-layouts: 10.7 us -> 0.88 us  [from_channels(): lax.all_to_all(arrange_map_over_axis(arranged, 0, 3), 'mp', split_axis=1,...]
    convert_element_type x1 -> x0, local copies, waits for them, and re-layouts: 9.63 us -> none  [body(): return from_channels((mixed[0] * total).astype(jnp.bfloat16))]
  transfers between devices with their start and end apart: 2 -> 2, of which waited for: 2 -> 2; matrix products, arithmetic and copies ran while one was open for 5% -> 7% of each run, Pallas kernels for 0% -> 0%
where the time goes in v1:
time: 189 us; the launch traced here: 187 us
  waiting for transfers between devices  63.5 us (34%)
  blocking collectives  44.1 us (23%)
  matrix products  41.5 us (22%)
  starting transfers between devices  18.4 us (10%)
  local copies, waits for them, and re-layouts  10.6 us (6%)
  other arithmetic  6.65 us (4%)
    all_to_all x1, waiting for transfers between devices, to_channels(): lax.all_to_all(arranged, 'seq', split_axis=1, concat_axis=4, tiled=True)  36.9 us
    all_to_all x1, waiting for transfers between devices, to_channels(): lax.all_to_all(lax.all_to_all(arranged, 'seq', split_axis=1, concat_axis=...  26.5 us
    all_to_all x1, blocking collectives, from_channels(): lax.all_to_all(arrange_map_over_axis(arranged, 0, 3), 'mp', split_axis=1,...  23.2 us
    all_to_all x1, blocking collectives, from_channels(): all_to_all(jnp.stack(jnp.split(arr_in, axis_size('seq'), axis=dim_at)), a...  20.9 us
    all_to_all x1, starting transfers between devices, to_channels(): lax.all_to_all(arranged, 'seq', split_axis=1, concat_axis=4, tiled=True)  11.2 us
    all_to_all x1, starting transfers between devices, to_channels(): lax.all_to_all(lax.all_to_all(arranged, 'seq', split_axis=1, concat_axis=...  7.21 us
    dot_general x2, matrix products, forward(): jnp.einsum('mcb,bd->mcd', turned_im, inner_table[0], precision=exact_mode)  6 us
    dot_general x2, matrix products, forward(): jnp.einsum('mcb,bd->mcd', turned_im, inner_table[1], precision=exact_mode)  5.66 us
  transfers between devices with their start and end apart: 2, of which 2 were waited for; matrix products, arithmetic and copies ran while one was open for 7% of the time, Pallas kernels for 0%

profile of v1, /device:TPU:33, one launch (start us, length us, event | category | flops | bytes accessed | tf_op | source)
XLA Modules:
  0.0 186.6 jit_solution(9444098533070855559)
XLA Ops:
  0.0 2.8 %copy.252 = bf16[3,64,4,8,128]{4,3,2,0,1:T(8,128)(2,1)} copy(bf16[3,64,4,8,128]{4,3,2,1,0:T(8,128)(2,1)} %bitcast.395) | data formatting | bytes 3145728 | tf_op jit(solution)/shard_map/reshape | solution.py:109
  2.8 11.2 %all-to-all-start = ((bf16[3,64,4,8,128]{4,3,2,0,1:T(8,128)(2,1)}), bf16[3,64,4,8,128]{4,3,2,0,1:T(8,128)(2,1)S(1)}, u32[]{:S(2)}, u32[]{:S(2)}) async-start(bf16[3,64,4,8,128]{4,3,2,0,1:T(8,128)(2,1)} %copy.252), calls=%async_computation | async-start | bytes 3145728 | tf_op jit(solution)/shard_map/all_to_all | solution.py:113
  14.2 36.9 %all-to-all-done = bf16[3,64,4,8,128]{4,3,2,0,1:T(8,128)(2,1)S(1)} async-done(((bf16[3,64,4,8,128]{4,3,2,0,1:T(8,128)(2,1)}), bf16[3,64,4,8,128]{4,3,2,0,1:T(8,128)(2,1)S(1)}, u32[]{:S(2)}, u32[]{:S(2)}) %all-to-all-start) | async-done | bytes 1572896 | tf_op jit(solution)/shard_map/all_to_all | solution.py:113
  51.7 2.1 %reshape.170 = bf16[3,1,4,8,8192]{4,3,0,1,2:T(8,128)(2,1)} reshape(bf16[3,1,4,8,64,128]{5,4,3,0,2,1:T(8,128)(2,1)S(1)} %copy.312) | data formatting | bytes 3145728 | tf_op jit(solution)/shard_map/all_to_all | solution.py:113
  53.8 7.2 %all-to-all-start.1 = ((bf16[3,1,4,8,8192]{4,3,0,1,2:T(8,128)(2,1)}), bf16[3,1,4,8,8192]{4,3,0,1,2:T(8,128)(2,1)S(1)}, u32[]{:S(2)}, u32[]{:S(2)}) async-start(bf16[3,1,4,8,8192]{4,3,0,1,2:T(8,128)(2,1)} %reshape.170), calls=%async_computation.1 | async-start | bytes 3145728 | tf_op jit(solution)/shard_map/all_to_all | solution.py:112
  61.0 3.3 %while.14 = (s32[]{:T(128)}, f32[8,8192]{1,0:T(8,128)S(1)}, f32[8,16]{0,1:T(8,128)S(1)}, f32[8,16]{0,1:T(8,128)S(1)}, s32[]{:T(128)}, /*index=5*/s32[]{:T(128)}) while((s32[]{:T(128)}, f32[8,8192]{1,0:T(8,128)S(1)}, f32[8,16]{0,1:T(8,128)S(1)}, f32[8,16]{0,1:T(8,128)S(1)}, s32[]{:T(128)}, /*index=5*/s32[]{:T(128)}) %tuple.40), condition=%wide.region_1.2_spmd.clone, body=%wide.region_0.1_spmd.clone.sunk | while | flops 262163 | bytes 524571 | solution.py:73
  70.3 2.0 %convolution_add_fusion.2 = f32[8,128,128]{2,1,0:T(8,128)} fusion(f32[8,128,128]{2,1,0:T(8,128)S(1)} %fusion.48, f32[8,128,128]{1,2,0:T(8,128)S(1)} %convolution_bitcast_fusion, f32[8,128,128]{1,2,0:T(8,128)S(1)} %convolution_bitcast_fusion.1, f32[128,128]{0,1:T(8,128)S(1)} %get-tuple-element.132, f32[128,128]{0,1:T(8,128)S(1)} %get-tuple-element.133), kind=kOutput, calls=%fused_computation.41 | convolution fusion | flops 202080256 | bytes 2228224 | tf_op jit(solution)/shard_map/mcb,bd->mcd/dot_general | solution.py:43
  72.3 2.0 %convolution_subtract_fusion.2 = f32[8,128,128]{2,1,0:T(8,128)} fusion(f32[8,128,128]{2,1,0:T(8,128)S(1)} %fusion.49, f32[8,128,128]{1,2,0:T(8,128)S(1)} %convolution_bitcast_fusion, f32[8,128,128]{1,2,0:T(8,128)S(1)} %convolution_bitcast_fusion.1, f32[128,128]{0,1:T(8,128)S(1)} %get-tuple-element.132, f32[128,128]{0,1:T(8,128)S(1)} %get-tuple-element.133), kind=kOutput, calls=%fused_computation.42 | convolution fusion | flops 202080256 | bytes 2228224 | tf_op jit(solution)/shard_map/mcb,bd->mcd/dot_general | solution.py:40
  74.3 26.5 %all-to-all-done.1 = bf16[3,1,4,8,8192]{4,3,0,1,2:T(8,128)(2,1)S(1)} async-done(((bf16[3,1,4,8,8192]{4,3,0,1,2:T(8,128)(2,1)}), bf16[3,1,4,8,8192]{4,3,0,1,2:T(8,128)(2,1)S(1)}, u32[]{:S(2)}, u32[]{:S(2)}) %all-to-all-start.1) | async-done | bytes 1572896 | tf_op jit(solution)/shard_map/all_to_all | solution.py:112
  101.2 1.7 multiply_add_fusion
  105.7 3.6 %fusion.44 = f32[32,128,128]{2,1,0:T(8,128)S(1)} fusion(f32[32,128,128]{2,1,0:T(8,128)S(1)} %fusion.92, f32[32,128,128]{2,1,0:T(8,128)S(1)} %fusion.91, f32[128,128]{0,1:T(8,128)S(1)} %get-tuple-element.132, f32[128,128]{0,1:T(8,128)S(1)} %get-tuple-element.133), kind=kOutput, calls=%fused_computation.55 | convolution fusion | flops 807108608 | bytes 6422528 | tf_op jit(solution)/shard_map/mcb,bd->mcd/dot_general | solution.py:38
  109.4 3.6 %fusion.42 = f32[32,128,128]{2,1,0:T(8,128)S(1)} fusion(f32[32,128,128]{2,1,0:T(8,128)S(1)} %fusion.92, f32[32,128,128]{2,1,0:T(8,128)S(1)} %fusion.91, f32[128,128]{0,1:T(8,128)S(1)} %get-tuple-element.132, f32[128,128]{0,1:T(8,128)S(1)} %get-tuple-element.133), kind=kOutput, calls=%fused_computation.54 | convolution fusion | flops 807108608 | bytes 6422528 | tf_op jit(solution)/shard_map/mcb,bd->mcd/dot_general | solution.py:41
  113.0 3.6 %convolution_subtract_fusion.1 = f32[32,128,128]{2,1,0:T(8,128)S(1)} fusion(f32[32,128,128]{2,1,0:T(8,128)S(1)} %fusion.44, f32[32,128,128]{2,1,0:T(8,128)S(1)} %fusion.92, f32[32,128,128]{2,1,0:T(8,128)S(1)} %fusion.91, f32[128,128]{0,1:T(8,128)S(1)} %get-tuple-element.132, f32[128,128]{0,1:T(8,128)S(1)} %get-tuple-element.133), kind=kOutput, calls=%fused_computation.32 | convolution fusion | flops 807632896 | bytes 8519680 | tf_op jit(solution)/shard_map/mcb,bd->mcd/dot_general | solution.py:40
  116.7 4.0 %fusion.6 = (f32[32,128,128]{2,1,0:T(8,128)S(1)}, f32[32,128,128]{2,1,0:T(8,128)S(1)}) fusion(f32[32,128,128]{2,1,0:T(8,128)S(1)} %convolution_subtract_fusion.1, f32[8,128,128]{2,1,0:T(8,128)S(1)} %copy-done, f32[8,128,128]{2,1,0:T(8,128)S(1)} %copy-done.1, f32[32,128,128]{2,1,0:T(8,128)S(1)} %fusion.42, f32[32,128,128]{2,1,0:T(8,128)S(1)} %fusion.92, ...), kind=kOutput, calls=%fused_computation.14 | convolution fusion | flops 810778624 | bytes 13762560 | tf_op jit(solution)/shard_map/mcb,bd->mcd/dot_general | solution.py:43
  120.7 2.3 %fusion.62 = f32[32,128,128]{1,2,0:T(8,128)S(1)} fusion(f32[32,128,128]{2,1,0:T(8,128)S(1)} %get-tuple-element.128), kind=kOutput, calls=%fused_computation.143 | convolution fusion | flops 805535744 | bytes 4194304 | tf_op jit(solution)/shard_map/mcd,bd->mcb/dot_general | solution.py:51
  123.0 2.3 %fusion.60 = f32[32,128,128]{1,2,0:T(8,128)S(1)} fusion(f32[32,128,128]{2,1,0:T(8,128)S(1)} %get-tuple-element.127), kind=kOutput, calls=%fused_computation.141 | convolution fusion | flops 805535744 | bytes 4194304 | tf_op jit(solution)/shard_map/mcd,bd->mcb/dot_general | solution.py:54
  125.3 2.3 %convolution_add_fusion = f32[32,128,128]{1,2,0:T(8,128)S(1)} fusion(f32[32,128,128]{1,2,0:T(8,128)S(1)} %fusion.62, f32[32,128,128]{2,1,0:T(8,128)S(1)} %get-tuple-element.127), kind=kOutput, calls=%fused_computation.30 | convolution fusion | flops 806060032 | bytes 6291456 | tf_op jit(solution)/shard_map/mcd,bd->mcb/dot_general | solution.py:51
  127.5 2.5 %convolution_subtract_fusion = f32[32,128,128]{1,2,0:T(8,128)S(1)} fusion(f32[32,128,128]{1,2,0:T(8,128)S(1)} %fusion.60, f32[32,128,128]{2,1,0:T(8,128)S(1)} %get-tuple-element.128), kind=kOutput, calls=%fused_computation.29 | convolution fusion | flops 806060032 | bytes 6291456 | tf_op jit(solution)/shard_map/mcd,bd->mcb/dot_general | solution.py:54
  130.1 2.6 %fusion.9 = f32[32,128,64]{1,2,0:T(8,128)S(1)} fusion(f32[32,128,128]{1,2,0:T(8,128)S(1)} %convolution_add_fusion, f32[32,128,128]{1,2,0:T(8,128)S(1)} %convolution_subtract_fusion, f32[128,128]{0,1:T(8,128)S(1)} %get-tuple-element.132, f32[128,128]{0,1:T(8,128)S(1)} %get-tuple-element.133, f32[128,128]{0,1:T(8,128)S(1)} %fusion.77), kind=kOutput, calls=%fused_computation.21 | convolution fusion | flops 404226048 | bytes 5406720 | tf_op jit(solution)/shard_map/ca,mcb->mab/dot_general | solution.py:61
  132.7 3.6 %fusion.29 = f32[32,64,128]{2,1,0:T(8,128)} fusion(f32[32,128,64]{1,2,0:T(8,128)S(1)} %fusion.9, f32[32,128,128]{1,2,0:T(8,128)S(1)} %convolution_subtract_fusion, f32[32,128,128]{1,2,0:T(8,128)S(1)} %convolution_add_fusion, f32[128,128]{0,1:T(8,128)S(1)} %get-tuple-element.132, f32[128,128]{0,1:T(8,128)S(1)} %get-tuple-element.133, f32[128,128]{0,1:T(8,128)S(1)} %fusion.78), kind=kOutput, calls=%fused_computation.38 | convolution fusion | flops 405274624 | bytes 6455296 | tf_op jit(solution)/shard_map/ca,mcb->mab/dot_general | solution.py:59
  136.4 2.4 %reshape.154 = f32[1,4,8,8192]{3,2,1,0:T(8,128)} reshape(f32[32,64,128]{2,1,0:T(8,128)} %fusion.29) | data formatting | bytes 2097152 | tf_op jit(solution)/shard_map/convert_element_type | solution.py:172
  138.8 1.5 fusion.34
  141.2 20.9 %all_to_all.33 = bf16[64,1,4,8,128]{4,3,2,1,0:T(8,128)(2,1)S(1)} all-to-all(bf16[64,1,4,8,128]{4,3,2,1,0:T(8,128)(2,1)S(1)} %constant_dynamic-update-slice_fusion), channel_id=1, replica_groups=mesh['seq'=64,'mp'=4] {'seq'}, dimensions={0} | all-to-all | bytes 1048576 | tf_op jit(solution)/shard_map/all_to_all | solution.py:128
  162.2 23.2 %all_to_all.34 = bf16[64,4,8,128]{3,2,0,1:T(8,128)(2,1)S(1)} all-to-all(bf16[64,4,8,128]{3,2,0,1:T(8,128)(2,1)S(1)} %copy.284), channel_id=1, replica_groups=mesh['seq'=64,'mp'=4] {'mp'}, dimensions={1} | all-to-all | bytes 1048576 | tf_op jit(solution)/shard_map/all_to_all | solution.py:136
  (132 shorter events, 13.7 us)
Async XLA Ops:
  2.8 11.3 %copy-start.4 = (f32[32,16]{0,1:T(8,128)S(1)}, f32[32,16]{0,1:T(8,128)}, u32[]{:S(2)}) copy-start(f32[32,16]{0,1:T(8,128)} %param.11) | copy-start | bytes 6148
  2.8 11.3 %copy-start.5 = (f32[32,16]{0,1:T(8,128)S(1)}, f32[32,16]{0,1:T(8,128)}, u32[]{:S(2)}) copy-start(f32[32,16]{0,1:T(8,128)} %param.10) | copy-start | bytes 6148
  2.8 48.3 %all-to-all-start = ((bf16[3,64,4,8,128]{4,3,2,0,1:T(8,128)(2,1)}), bf16[3,64,4,8,128]{4,3,2,0,1:T(8,128)(2,1)S(1)}, u32[]{:S(2)}, u32[]{:S(2)}) async-start(bf16[3,64,4,8,128]{4,3,2,0,1:T(8,128)(2,1)} %copy.252), calls=%async_computation | async-start | bytes 3145728 | tf_op jit(solution)/shard_map/all_to_all | solution.py:113
  53.8 47.1 %all-to-all-start.1 = ((bf16[3,1,4,8,8192]{4,3,0,1,2:T(8,128)(2,1)}), bf16[3,1,4,8,8192]{4,3,0,1,2:T(8,128)(2,1)S(1)}, u32[]{:S(2)}, u32[]{:S(2)}) async-start(bf16[3,1,4,8,8192]{4,3,0,1,2:T(8,128)(2,1)} %reshape.170), calls=%async_computation.1 | async-start | bytes 3145728 | tf_op jit(solution)/shard_map/all_to_all | solution.py:112
  61.0 3.3 %copy-start.2 = (f32[3,3,8192]{2,1,0:T(4,128)S(1)}, f32[3,3,8192]{2,1,0:T(4,128)}, u32[]{:S(2)}) copy-start(f32[3,3,8192]{2,1,0:T(4,128)} %param.8) | copy-start | bytes 884740
  61.0 3.9 %copy-start.3 = (f32[8192]{0:T(1024)S(1)}, f32[8192]{0:T(1024)}, u32[]{:S(2)}) copy-start(f32[8192]{0:T(1024)} %param.9) | copy-start | bytes 98308
  113.0 3.7 %copy-start = (f32[8,128,128]{2,1,0:T(8,128)S(1)}, f32[8,128,128]{2,1,0:T(8,128)}, u32[]{:S(2)}) copy-start(f32[8,128,128]{2,1,0:T(8,128)} %convolution_add_fusion.2) | copy-start | bytes 1572868
  113.0 3.7 %copy-start.1 = (f32[8,128,128]{2,1,0:T(8,128)S(1)}, f32[8,128,128]{2,1,0:T(8,128)}, u32[]{:S(2)}) copy-start(f32[8,128,128]{2,1,0:T(8,128)} %convolution_subtract_fusion.2) | copy-start | bytes 1572868
